TPU v7x, 128 devices: a whole 4x4x4 slice. The times are simulated.
128 devices in a mesh: row: 8 (over z_lo, y), col: 16 (over z_hi, x, core).
Axes of the slice: x: 4, y: 4, z: 4 (z_hi: 2, z_lo: 2; z = z_hi * 2 + z_lo), core: 2. Of those that a mesh axis runs over, the one named last changes fastest.
Arguments:
- slip: float32 [262144, 256], P(('row', 'col')), may hold values from -2 to 2
- state: float32 [262144, 256], P(('row', 'col')), may hold values from 0.4 to 0.9
- tau_load: float32 [262144], P(('row', 'col')), may hold values from 1 to 2
- normal_stress: float32 [262144], P(('row', 'col')), may hold values from 6 to 8
- direct_effect: float32 [262144], P(('row', 'col')), may hold values from 0.8 to 1.6
- evolution_effect: float32 [262144], P(('row', 'col')), may hold values from 0.5 to 1
- slip_distance: float32 [262144], P(('row', 'col')), may hold values from 0.5 to 2
- self_stiffness: float32 [262144], P(('row', 'col')), may hold values from 0.5 to 2
- near_blocks: bfloat16 [3, 262144, 256], P(None, ('row', 'col')), may hold values from -0.21875 to 0.21875
- basis_in: bfloat16 [32, 262144], P(None, ('row', 'col')), may hold values from -0.375 to 0.375
- basis_out: bfloat16 [32, 262144], P(None, ('row', 'col')), may hold values from -1 to 1
- coupling: bfloat16 [32768, 8, 4096], P('row', None, 'col'), may hold values from -0.046875 to 0.046875
- block_rank: int32 [1024, 8, 128], P('row', None, 'col'), may hold values from 8 to 32
- adj_bricks: int32 [8, 262144], P(None, ('row', 'col')), may hold values from 0 to 2047
- adj_count: int32 [262144], P(('row', 'col')), may hold values from 1 to 8
- adj_weight: float32 [8, 262144], P(None, ('row', 'col')), may hold values from 0.05 to 1
- pressure_now: bfloat16 [2048, 256], P('col'), may hold values from 0.099609375 to 1
- pressure_rate: bfloat16 [2048, 256], P('col'), may hold values from 0.5 to 5
Outputs:
- slip_out: float32 [262144, 256], P(('row', 'col'))
- state_out: float32 [262144, 256], P(('row', 'col'))
Inputs may be any that keep to these rules, and one draw needn't show every extreme that they name: Only the first adj_count entries of a patch's brick list are read. `adj_bricks`: brick numbers index the whole reservoir. `block_rank`: ranks of pairs with |i - j| <= 1 are not read.
All inputs are finite; a program needn't handle non-finite values.
Results may differ from a plain program's by a relative error of at most 0.0007.
Values may be sent and summed in bfloat16 or wider, within the bound.
A program may use at most 192 MiB of HBM per device.

v0:
```python
import jax
import jax.numpy as jnp
from jax import lax
from jax.sharding import PartitionSpec as P

BS = 256
R = 32
BPD = 8


STEP_SIZE = 0.5
REF_FRICTION = 0.6


def with_halo(array, sides, width):
    for axis, dim in sides:
        devices, length = (lax.axis_size(axis), array.shape[dim])
        up = [(i, (i + 1) % devices) for i in range(devices - 1)]
        down = [(j, i) for i, j in up]
        last = lax.slice_in_dim(array, length - width, length, axis=dim)
        initial = lax.slice_in_dim(array, 0, width, axis=dim)
        before = lax.ppermute(last, axis, up)
        after = lax.ppermute(initial, axis, down)
        array = jnp.concatenate([before, array, after], axis=dim)
    return array


def fault_pressure(joined, adj_bricks, adj_count, adj_weight):
    slots = adj_bricks.shape[0]
    patches = adj_bricks.shape[1]
    slot_ids = jnp.arange(slots, dtype=jnp.int32)
    live = (adj_count[None, :] > slot_ids[:, None]).astype(jnp.float32)
    weighting = adj_weight * live
    weight_sum = jnp.sum(weighting, axis=0)
    picked = joined[adj_bricks.reshape(slots * patches)].reshape(slots, patches, joined.shape[1])
    total = jnp.sum(weighting[:, :, None] * picked.astype(jnp.float32), axis=0)
    return total / weight_sum[:, None]


def far_mask_flat(row_blocks, col_blocks, ranks):
    row_total = row_blocks.shape[0]
    col_total = col_blocks.shape[0]
    row_block_of = jnp.repeat(row_blocks, R)
    col_block_of = jnp.repeat(col_blocks, R)
    row_level = jnp.arange(row_total * R, dtype=jnp.int32) % R
    col_level = jnp.arange(col_total * R, dtype=jnp.int32) % R
    spread = (
        jnp.arange(col_total, dtype=jnp.int32)[:, None]
        == (jnp.arange(col_total * R, dtype=jnp.int32) // R)[None, :]
    ).astype(jnp.float32)
    rank_cols = jnp.dot(
        ranks.astype(jnp.float32),
        spread,
        precision=lax.Precision.HIGHEST,
        preferred_element_type=jnp.float32,
    )
    rank_full = jnp.broadcast_to(rank_cols[:, None, :], (row_total, R, col_total * R)).reshape(
        row_total * R, col_total * R
    )
    level = jnp.maximum(row_level[:, None], col_level[None, :]).astype(jnp.float32)
    apart = jnp.abs(row_block_of[:, None] - col_block_of[None, :]) > 1
    return apart & (level < rank_full)


def rates(
    slip_now,
    state_now,
    outer,
    pressure,
    tau_load,
    normal_stress,
    direct_effect,
    evolution_effect,
    slip_distance,
    self_stiffness,
):
    tau = tau_load[:, None] - self_stiffness[:, None] * slip_now - outer
    sigma = normal_stress[:, None] - pressure
    speed = jnp.exp((tau / sigma - state_now) / direct_effect[:, None])
    drift = (evolution_effect / slip_distance)[:, None] * (
        jnp.exp((REF_FRICTION - state_now) / evolution_effect[:, None]) - speed
    )
    return (speed, drift)


def project(basis, slips):
    count = slips.shape[0] // BS
    coeff = jnp.einsum(
        "rnb,nbe->nre",
        basis.reshape(R, count, BS),
        slips.reshape(count, BS, slips.shape[1]),
        preferred_element_type=jnp.float32,
    )
    return coeff.astype(jnp.bfloat16).reshape(count * R, slips.shape[1])


def near_field(padded, near_blocks):
    patches = near_blocks.shape[1]
    count = patches // BS
    terms = []
    for neighbour in range(3):
        window = padded[neighbour * BS : neighbour * BS + patches].reshape(
            count, BS, padded.shape[1]
        )
        terms.append(
            jnp.einsum(
                "gns,gsl->gnl",
                near_blocks[neighbour].reshape(count, BS, BS),
                window,
                preferred_element_type=jnp.float32,
            )
        )
    return (terms[0] + terms[1] + terms[2]).reshape(patches, padded.shape[1])


def per_device(
    slip,
    state,
    tau_load,
    normal_stress,
    direct_effect,
    evolution_effect,
    slip_distance,
    self_stiffness,
    near_blocks,
    basis_in,
    basis_out,
    coupling,
    block_rank,
    adj_bricks,
    adj_count,
    adj_weight,
    pressure_now,
    pressure_rate,
):
    now_all, rate_all = (
        lax.all_gather(pressure_now, "col", axis=0, tiled=True),
        lax.all_gather(pressure_rate, "col", axis=0, tiled=True),
    )
    scenarios = slip.shape[1]
    joined = jnp.concatenate([now_all, rate_all], 1)
    both_press = fault_pressure(joined, adj_bricks, adj_count, adj_weight)
    base_press = both_press[:, :scenarios]
    rate_press = both_press[:, scenarios:]
    row_count = lax.axis_size("row")
    col_count = lax.axis_size("col")
    row_index = lax.axis_index("row")
    col_index = lax.axis_index("col")
    matrix = coupling.reshape(coupling.shape[0], coupling.shape[1] * coupling.shape[2])
    ranks = block_rank.reshape(block_rank.shape[0], block_rank.shape[1] * block_rank.shape[2])
    row_blocks = row_index * (col_count * BPD) + jnp.arange(col_count * BPD, dtype=jnp.int32)
    source_rows = jnp.arange(row_count, dtype=jnp.int32)[:, None] * col_count + col_index
    col_blocks = (source_rows * BPD + jnp.arange(BPD, dtype=jnp.int32)[None, :]).reshape(
        row_count * BPD
    )
    keep = far_mask_flat(row_blocks, col_blocks, ranks)
    masked = jnp.where(keep, matrix, jnp.zeros((), jnp.bfloat16))
    share = BPD * R
    basis_all = lax.all_gather(basis_in, "row", axis=1, tiled=True)

    def stress(slip_now):
        rounded = slip_now.astype(jnp.bfloat16)
        slip_all = lax.all_gather(rounded, "row", axis=0, tiled=True)
        coeff = project(basis_all, slip_all)
        partial_sum = jnp.dot(masked, coeff, preferred_element_type=jnp.float32)
        total = lax.psum(partial_sum.astype(jnp.bfloat16), "col").astype(jnp.float32)
        mine = lax.dynamic_slice_in_dim(total, col_index * share, share, 0)
        far_coeff = mine.astype(jnp.bfloat16)
        far = jnp.einsum(
            "rnb,nre->nbe",
            basis_out.reshape(R, BPD, BS),
            far_coeff.reshape(BPD, R, slip_now.shape[1]),
            preferred_element_type=jnp.float32,
        )
        far = far.reshape(slip_now.shape)
        padded = with_halo(rounded, ((("row", "col"), 0),), BS)
        near = near_field(padded, near_blocks)
        return near + far

    params = (
        tau_load,
        normal_stress,
        direct_effect,
        evolution_effect,
        slip_distance,
        self_stiffness,
    )
    speed0, drift0 = rates(slip, state, stress(slip), base_press, *params)
    slip_mid = slip + STEP_SIZE * speed0
    state_mid = state + STEP_SIZE * drift0
    speed1, drift1 = rates(
        slip_mid, state_mid, stress(slip_mid), base_press + STEP_SIZE * rate_press, *params
    )
    slip_out = slip + 0.5 * STEP_SIZE * (speed0 + speed1)
    state_out = state + 0.5 * STEP_SIZE * (drift0 + drift1)
    return (slip_out, state_out)


def solution(mesh):
    in_specs = (
        P(("row", "col"), None),
        P(("row", "col"), None),
        P(("row", "col")),
        P(("row", "col")),
        P(("row", "col")),
        P(("row", "col")),
        P(("row", "col")),
        P(("row", "col")),
        P(None, ("row", "col"), None),
        P(None, ("row", "col")),
        P(None, ("row", "col")),
        P("row", None, "col"),
        P("row", None, "col"),
        P(None, ("row", "col")),
        P(("row", "col")),
        P(None, ("row", "col")),
        P("col", None),
        P("col", None),
    )
    out_specs = (P(("row", "col"), None), P(("row", "col"), None))
    return jax.shard_map(
        per_device, mesh=mesh, in_specs=in_specs, out_specs=out_specs, check_vma=False
    )
```

profile of v0, /device:TPU:1, one launch (start us, length us, event | category | flops | bytes accessed | tf_op | source)
XLA Modules:
  0.0 662.5 jit_solution(3476036359275173559)
XLA Ops:
  7.2 0.7 all-gather.6.cloned.1.call-update
  8.0 2.7 convert_element_type.52
  10.6 0.0 all-gather.10.cloned.1.call-start
  10.7 0.7 all-gather.10.cloned.1.call-update
  11.4 1.0 fusion.43
  12.4 4.5 collective-permute-start
  16.9 1.9 collective-permute-start.1
  18.9 0.0 all-reduce.3.cloned.1.call-start
  19.0 0.1 iota_add_fusion
  19.1 0.1 broadcast_in_dim.12
  19.1 0.1 broadcast_in_dim.13
  19.2 0.1 broadcast_in_dim.11
  19.3 0.1 sub.77
  19.4 1.0 convolution_bitcast_fusion
  20.4 0.3 copy.23
  20.7 11.4 %broadcast_in_dim.14 = f32[128,32,2048]{2,1,0:T(8,128)} broadcast(f32[128,2048]{1,0:T(8,128)S(1)} %copy.23), dimensions={0,2} | broadcast | bytes 34603008 | tf_op jit(solution)/shard_map/broadcast_in_dim | solution.py:57
  32.1 19.9 %copy.30 = f32[512,8,8,256]{3,2,1,0:T(8,128)S(1)} copy(f32[512,8,8,256]{3,1,2,0:T(8,128)} %bitcast.99) | data formatting | bytes 67108864
  52.1 22.4 %fusion.2 = bf16[4096,8,256]{2,1,0:T(8,128)(2,1)} fusion(bf16[4096,8,256]{2,1,0:T(8,128)(2,1)} %param.29, f32[512,8,8,256]{3,2,1,0:T(8,128)S(1)} %copy.30, s32[8,256]{1,0:T(8,128)S(1)} %add_select_fusion.2, s32[4096]{0:T(1024)S(1)} %add_select_fusion, s32[8,256]{1,0:T(8,128)S(1)} %broadcast_in_dim.13, s32[4096]{0:T(1024)S(1)} %sub.77), kind=kLoop, calls=%fused_computation.6 | loop fusion | flops 67108864 | bytes 67158016 | tf_op jit(solution)/shard_map/jit(_where)/select_n | solution.py:157
  74.5 16.5 %copy.31 = bf16[512,8,8,256]{3,1,2,0:T(8,128)(2,1)} copy(bf16[512,8,8,256]{3,2,1,0:T(8,128)(2,1)} %bitcast.101) | data formatting | bytes 33554432
  91.0 1.2 fusion.41
  92.1 0.1 copy.32
  92.2 0.1 compare_select_fusion
  92.3 0.2 copy-done.3
  92.5 3.4 fusion.44
  96.0 2.1 pad_maximum_fusion.3
  98.0 1.8 fusion.45
  99.9 45.0 %all-gather.8.cloned.1.call-done = bf16[16384,256]{1,0:T(8,128)(2,1)} async-done(((bf16[2048,256]{1,0:T(8,128)(2,1)}), bf16[16384,256]{1,0:T(8,128)(2,1)}) %all-gather.8.cloned.1.call-update) | async-done | bytes 8388624 | tf_op jit(solution)/shard_map/all_gather | solution.py:163
  144.8 5.2 convolution_convert_fusion.3
  150.0 9.6 %convolution_convert_fusion.1 = bf16[4096,256]{1,0:T(8,128)(2,1)} fusion(bf16[4096,2048]{1,0:T(8,128)(2,1)} %bitcast.106, bf16[2048,256]{1,0:T(8,128)(2,1)S(1)} %bitcast.121), kind=kOutput, calls=%fused_computation.8 | convolution fusion | flops 4296015872 | bytes 19922944 | tf_op jit(solution)/shard_map/dot_general | solution.py:165
  159.7 0.2 all-gather.14.cloned.1.call-start
  159.9 31.6 %all-gather.10.cloned.1.call-done = bf16[2048,256]{1,0:T(8,128)(2,1)} async-done(((bf16[128,256]{1,0:T(8,128)(2,1)}), bf16[2048,256]{1,0:T(8,128)(2,1)}) %all-gather.10.cloned.1.call-update) | async-done | bytes 1048592 | tf_op jit(solution)/shard_map/all_gather | solution.py:137
  191.5 45.9 %all-gather.12.cloned.1.call-done = bf16[2048,256]{1,0:T(8,128)(2,1)} async-done(((bf16[128,256]{1,0:T(8,128)(2,1)}), bf16[2048,256]{1,0:T(8,128)(2,1)}) %all-gather.12.cloned.1.call-update) | async-done | bytes 1048592 | tf_op jit(solution)/shard_map/all_gather | solution.py:138
  237.4 1.7 pad_maximum_fusion
  239.1 66.4 %gather_fusion = bf16[16384,512]{1,0:T(8,128)(2,1)} fusion(bf16[2048,512]{1,0:T(8,128)(2,1)S(1)} %pad_maximum_fusion, s32[16384]{0:T(1024)S(1)} %broadcast_clamp_fusion), kind=kCustom, calls=%fused_computation | custom fusion | bytes 33619968 | tf_op jit(solution)/shard_map/gather | solution.py:35
  305.5 7.5 %fusion = f32[2048,512]{1,0:T(8,128)S(1)} fusion(bf16[8,2048,512]{2,1,0:T(8,128)(2,1)} %bitcast.100, f32[8,2048]{1,0:T(8,128)S(1)} %get-tuple-element.7), kind=kLoop, calls=%fused_computation.3 | loop fusion | flops 24117248 | bytes 21037056 | tf_op jit(solution)/shard_map/reduce_sum | solution.py:36
  313.1 2.4 broadcast_divide_fusion
  315.5 67.4 %all-reduce.3.cloned.1.call-done = bf16[4096,256]{1,0:T(8,128)(2,1)} async-done(((bf16[4096,256]{1,0:T(8,128)(2,1)}), bf16[4096,256]{1,0:T(8,128)(2,1)}) %all-reduce.3.cloned.1.call-update) | async-done | bytes 2097168 | tf_op jit(solution)/shard_map/psum | solution.py:166
  382.9 1.1 convert_convert_fusion.1
  384.0 0.5 fusion.21
  384.5 0.1 copy-done.11
  384.6 2.8 bitcast_add_fusion
  387.4 0.9 copy-done.1
  388.3 0.6 copy-done.12
  388.9 3.4 fusion.15
  392.4 93.1 %all-gather.14.cloned.1.call-done = bf16[16384,256]{1,0:T(8,128)(2,1)} async-done(((bf16[2048,256]{1,0:T(8,128)(2,1)}), bf16[16384,256]{1,0:T(8,128)(2,1)}) %all-gather.14.cloned.1.call-update) | async-done | bytes 8388624 | tf_op jit(solution)/shard_map/all_gather | solution.py:163
  485.5 4.8 convolution_convert_fusion.2
  490.3 9.7 %convolution_convert_fusion = bf16[4096,256]{1,0:T(8,128)(2,1)} fusion(bf16[4096,2048]{1,0:T(8,128)(2,1)} %bitcast.107, bf16[2048,256]{1,0:T(8,128)(2,1)S(1)} %bitcast.120), kind=kOutput, calls=%fused_computation.7 | convolution fusion | flops 4296015872 | bytes 19922944 | tf_op jit(solution)/shard_map/dot_general | solution.py:165
  500.0 0.7 copy-done.19
  500.7 0.5 copy-done.4
  501.2 3.8 collective-permute-start.2
  505.1 1.9 collective-permute-start.3
  507.0 3.1 fusion.47
  510.1 2.6 collective-permute-done.3
  512.6 1.1 pad_maximum_fusion.2
  513.7 1.8 fusion.46
  515.5 127.8 %all-reduce.5.cloned.1.call-done = bf16[4096,256]{1,0:T(8,128)(2,1)} async-done(((bf16[4096,256]{1,0:T(8,128)(2,1)}), bf16[4096,256]{1,0:T(8,128)(2,1)}) %all-reduce.5.cloned.1.call-update) | async-done | bytes 2097168 | tf_op jit(solution)/shard_map/psum | solution.py:166
  643.3 1.0 convert_convert_fusion
  644.3 0.5 fusion.19
  644.9 2.9 add_add_fusion
  647.8 0.5 copy-done.2
  648.3 0.7 copy-done.5
  649.0 0.6 copy-done.13
  649.6 4.3 multiply_add_fusion
  653.9 1.7 multiply_add_fusion.1
  (67 shorter events, 0.4 us)
Async XLA Ops:
  7.2 92.7 %all-gather.6.cloned.1.call-start = ((), (), s32[]{:S(2)}) async-start(), calls=%async_computation | async-start | bytes 1179648 | tf_op jit(solution)/shard_map/all_gather | solution.py:159
  7.9 11.5 %copy-start.24 = (s32[128,8,8]{0,2,1:T(8,128)S(1)}, s32[128,8,8]{0,2,1:T(8,128)}, u32[]{:S(2)}) copy-start(s32[128,8,8]{0,2,1:T(8,128)} %param.30) | copy-start | bytes 98308
  7.9 136.9 %all-gather.8.cloned.1.call-start = ((), (), s32[]{:S(2)}) async-start(), calls=%async_computation.1 | async-start | bytes 9437184 | tf_op jit(solution)/shard_map/all_gather | solution.py:163
  10.6 180.9 %all-gather.10.cloned.1.call-start = ((), (), s32[]{:S(2)}) async-start(), calls=%async_computation.3 | async-start | bytes 1114112 | tf_op jit(solution)/shard_map/all_gather | solution.py:137
  11.4 226.0 %all-gather.12.cloned.1.call-start = ((), (), s32[]{:S(2)}) async-start(), calls=%async_computation.4 | async-start | bytes 1114112 | tf_op jit(solution)/shard_map/all_gather | solution.py:138
  12.4 83.5 %collective-permute-start = (bf16[256,256]{1,0:T(8,128)(2,1)S(1)}, bf16[256,256]{1,0:T(8,128)(2,1)}, u32[]{:S(2)}, u32[]{:S(2)}) collective-permute-start(bf16[256,256]{1,0:T(8,128)(2,1)S(1)} %get-tuple-element.18), channel_id=1, source_target_pairs={{0,1},{1,2},{2,3},{3,4},{4,5},{5,6},{6,7},{7,8},{8,9},{9,10},{10,1... | collective-permute-start | bytes 393224 | tf_op jit(solution)/shard_map/ppermute | solution.py:22
  16.9 79.0 %collective-permute-start.1 = (bf16[256,256]{1,0:T(8,128)(2,1)S(1)}, bf16[256,256]{1,0:T(8,128)(2,1)}, u32[]{:S(2)}, u32[]{:S(2)}) collective-permute-start(bf16[256,256]{1,0:T(8,128)(2,1)S(1)} %get-tuple-element.17), channel_id=1, source_target_pairs={{1,0},{2,1},{3,2},{4,3},{5,4},{6,5},{7,6},{8,7},{9,8},{10,9},{11,1... | collective-permute-start | bytes 393224 | tf_op jit(solution)/shard_map/ppermute | solution.py:23
  18.9 364.0 %all-reduce.3.cloned.1.call-start = ((), (), s32[]{:S(2)}) async-start(), calls=%async_computation.2 | async-start | bytes 4194304 | tf_op jit(solution)/shard_map/psum | solution.py:166
  74.5 16.5 %copy-start.15 = (bf16[3,2048,256]{2,1,0:T(8,128)(2,1)S(1)}, bf16[3,2048,256]{2,1,0:T(8,128)(2,1)}, u32[]{:S(2)}) copy-start(bf16[3,2048,256]{2,1,0:T(8,128)(2,1)} %param.26) | copy-start | bytes 9437188
  91.0 1.2 copy-start.17
  91.0 1.6 copy-start.3
  92.1 5.9 copy-start.9
  92.1 292.3 %copy-start.7 = (bf16[1,2048,256]{2,1,0:T(8,128)(2,1)}, bf16[1,2048,256]{2,1,0:T(8,128)(2,1)S(1)}, u32[]{:S(2)}) copy-start(bf16[1,2048,256]{2,1,0:T(8,128)(2,1)S(1)} %get-tuple-element.8) | copy-start | bytes 3145732
  92.5 3.4 copy-start.18
  92.5 3.4 copy-start.25
  159.7 325.8 %all-gather.14.cloned.1.call-start = ((), (), s32[]{:S(2)}) async-start(), calls=%async_computation.5 | async-start | bytes 9437184 | tf_op jit(solution)/shard_map/all_gather | solution.py:163
  313.1 70.9 %copy-start.16 = (bf16[32,2048]{1,0:T(8,128)(2,1)S(1)}, bf16[32,2048]{1,0:T(8,128)(2,1)}, u32[]{:S(2)}) copy-start(bf16[32,2048]{1,0:T(8,128)(2,1)} %param.28) | copy-start | bytes 393220
  382.9 1.7 copy-start.11
  384.5 2.8 copy-start
  384.5 3.8 copy-start.1
  384.5 4.4 copy-start.12
  384.5 4.4 copy-start.20
  384.5 4.4 copy-start.21
  384.6 4.4 copy-start.22
  384.6 4.4 copy-start.23
  392.3 93.1 %copy-start.6 = (bf16[32,16384]{1,0:T(8,128)(2,1)S(1)}, bf16[32,16384]{1,0:T(8,128)(2,1)}, u32[]{:S(2)}) copy-start(bf16[32,16384]{1,0:T(8,128)(2,1)} %all-gather.6.cloned.1.call-done) | copy-start | bytes 3145732
  392.4 251.0 %all-reduce.5.cloned.1.call-start = ((), (), s32[]{:S(2)}) async-start(), calls=%async_computation.6 | async-start | bytes 4194304 | tf_op jit(solution)/shard_map/psum | solution.py:166
  499.9 0.7 copy-start.19
  500.0 0.7 copy-start.26
  500.0 1.3 copy-start.4
  501.2 8.8 %collective-permute-start.2 = (bf16[256,256]{1,0:T(8,128)(2,1)S(1)}, bf16[256,256]{1,0:T(8,128)(2,1)S(1)}, u32[]{:S(2)}, u32[]{:S(2)}) collective-permute-start(bf16[256,256]{1,0:T(8,128)(2,1)S(1)} %get-tuple-element.13), channel_id=1, source_target_pairs={{0,1},{1,2},{2,3},{3,4},{4,5},{5,6},{6,7},{7,8},{8,9},{9,10},{10,1... | collective-permute-start | bytes 393224 | tf_op jit(solution)/shard_map/ppermute | solution.py:22
  505.1 7.6 %collective-permute-start.3 = (bf16[256,256]{1,0:T(8,128)(2,1)S(1)}, bf16[256,256]{1,0:T(8,128)(2,1)S(1)}, u32[]{:S(2)}, u32[]{:S(2)}) collective-permute-start(bf16[256,256]{1,0:T(8,128)(2,1)S(1)} %get-tuple-element.14), channel_id=1, source_target_pairs={{1,0},{2,1},{3,2},{4,3},{5,4},{6,5},{7,6},{8,7},{9,8},{10,9},{11,1... | collective-permute-start | bytes 393224 | tf_op jit(solution)/shard_map/ppermute | solution.py:23
  510.1 3.7 copy-start.10
  515.5 129.3 %copy-start.8 = (bf16[1,2048,256]{2,1,0:T(8,128)(2,1)S(1)}, bf16[1,2048,256]{2,1,0:T(8,128)(2,1)}, u32[]{:S(2)}) copy-start(bf16[1,2048,256]{2,1,0:T(8,128)(2,1)} %copy-done.7) | copy-start | bytes 3145732
  643.3 1.5 copy-start.14
  644.8 3.5 copy-start.2
  644.8 4.1 copy-start.5
  644.9 4.7 copy-start.13
Sparse Core Ops, SparseCore 0:
  9.6 36.9 all-gather.5
  48.8 95.9 all-gather.7
  147.3 44.1 all-gather.9
  193.8 43.5 all-gather.11
  240.3 142.5 all-reduce.2
  392.5 92.9 all-gather.13
  500.1 143.1 all-reduce.4
where the time goes:
time: 663 us; the launch traced here: 662 us
  waiting for transfers between devices  415 us (63%)
  local copies, waits for them, and re-layouts  122 us (18%)
  other arithmetic  51.6 us (8%)
  matrix products  47 us (7%)
  between operations  14.5 us (2%)
  starting transfers between devices  12.6 us (2%)
    psum x2, waiting for transfers between devices, stress(): lax.psum(partial_sum.astype(jnp.bfloat16), 'col').astype(jnp.float32)  195 us
    all_gather x2, waiting for transfers between devices, stress(): slip_all = lax.all_gather(rounded, 'row', axis=0, tiled=True)  138 us
    gather x1, local copies, waits for them, and re-layouts, fault_pressure(): joined[adj_bricks.reshape(slots * patches)]  66.4 us
    all_gather x1, waiting for transfers between devices, per_device(): lax.all_gather(pressure_rate, 'col', axis=0, tiled=True)  45.9 us
    unnamed x57, local copies, waits for them, and re-layouts  41.4 us
    all_gather x1, waiting for transfers between devices, per_device(): lax.all_gather(pressure_now, 'col', axis=0, tiled=True)  31.6 us
    select_n x1, other arithmetic, per_device(): masked = jnp.where(keep, matrix, jnp.zeros((), jnp.bfloat16))  22.4 us
    dot_general x2, matrix products, stress(): partial_sum = jnp.dot(masked, coeff, preferred_element_type=jnp.float32)  19.3 us
  transfers between devices with their start and end apart: 11, of which 7 were waited for; matrix products, arithmetic and copies ran while one was open for 28% of the time, Pallas kernels for 0%

commit v1 on v0

v1 whole, which is shorter than its diff:
```python
import jax
import jax.numpy as jnp
from jax import lax
from jax.experimental import pallas as pl
from jax.experimental.pallas import tpu as pltpu
from jax.sharding import PartitionSpec as P

BS = 256
R = 32
BPD = 8
NPAT = 2048
ENS = 256
STEP_SIZE = 0.5
REF_FRICTION = 0.6
BF = jnp.bfloat16
F32 = jnp.float32
MESH = pl.DeviceIdType.MESH


def rows(start, size):
    return pl.ds(pl.multiple_of(start, size), size)


def kernel(
    slip_h, state_h, par_h, near_h, bin_h, bout_h, coup_h, rank_h, adj_h, adjw_h, now_h, rate_h,
    slip_o, state_o,
    cm, rm, buf, pm, rank, slip, state, nb, bin_, bout, adj, adjw, par, cols, tab, wb, press,
    s0, s1, co0, co1, part, rx0, rx1, snd, rcv0, rcv1, fc, acc_s, acc_t,
    lsem, csem, osem, a_s, a_r, h_s, h_r, p_s, p_r, p2_s, p2_r, b1_s, b1_r, b2_s, b2_r,
):
    row = lax.axis_index("row")
    col = lax.axis_index("col")
    core = lax.rem(col, 2)
    q = col // 2
    g = row * 16 + col
    partner = (row, q * 2 + 1 - core)
    after = lax.rem(g + 1, 128)
    before = lax.rem(g + 127, 128)
    after = (after // 16, lax.rem(after, 16))
    before = (before // 16, lax.rem(before, 16))
    row_peers = [(lax.rem(row + j, 8), col) for j in range(1, 8)]
    col_peers = [(row, lax.rem(q + j, 8) * 2 + core) for j in range(1, 8)]

    def remote(src, dst, send, recv, device):
        return pltpu.make_async_remote_copy(
            src_ref=src, dst_ref=dst, send_sem=send, recv_sem=recv, device_id=device, device_id_type=MESH
        )

    barrier = pltpu.get_barrier_semaphore()
    for peer in row_peers + col_peers + [partner, after, before]:
        pl.semaphore_signal(barrier, inc=1, device_id=peer, device_id_type=MESH)

    def chunk(j):
        slot = lax.rem(j, 4)
        return pltpu.make_async_copy(coup_h.at[rows(j * 1024, 1024)], buf.at[slot], csem.at[slot])

    load = {}

    def start(name, src, dst, index):
        load[name] = pltpu.make_async_copy(src, dst, lsem.at[index])
        load[name].start()

    start("slip", slip_h, slip, 0)
    start("bin", bin_h, bin_, 1)
    start("now", now_h, tab.at[q, core, :, pl.ds(0, 256)], 2)
    start("rate", rate_h, tab.at[q, core, :, pl.ds(256, 256)], 3)
    start("rank", rank_h, rank, 4)
    for j in range(3):
        chunk(j).start()
    start("par", par_h, par, 5)
    start("adj", adj_h, adj, 6)
    start("adjw", adjw_h, adjw, 7)
    start("bout", bout_h, bout, 8)

    def project(field, co, b):
        block = field[pl.ds(pl.multiple_of(b * BS + BS, BS), BS)]
        out = jnp.dot(bin_[:, rows(b * BS, BS)], block, preferred_element_type=F32)
        co[b // 4, row, rows(lax.rem(b, 4) * R, R)] = out.astype(BF)

    def gather_copies(stage, co, half):
        return [
            remote(co.at[half, row], co.at[half, row], a_s.at[stage, half, j], a_r.at[stage, half, row], row_peers[j])
            for j in range(7)
        ]

    def gather_waits(stage, co, half):
        for j in range(1, 8):
            u = lax.rem(row + 8 - j, 8)
            remote(co.at[half, u], co.at[half, u], a_s.at[stage, half, 0], a_r.at[stage, half, u], row_peers[0]).wait_recv()

    def halo_copies(stage, field):
        return [
            remote(field.at[pl.ds(BS, BS)], field.at[pl.ds(9 * BS, BS)], h_s.at[stage, 0], h_r.at[stage, 0], before),
            remote(field.at[pl.ds(8 * BS, BS)], field.at[pl.ds(0, BS)], h_s.at[stage, 1], h_r.at[stage, 1], after),
        ]

    def halo_waits(copies, field):
        for copy in copies:
            copy.wait_recv()

        @pl.when(g == 0)
        def _():
            field[pl.ds(0, BS)] = jnp.zeros((BS, ENS), BF)

        @pl.when(g == 127)
        def _():
            field[pl.ds(9 * BS, BS)] = jnp.zeros((BS, ENS), BF)

    load["slip"].wait()
    load["bin"].wait()

    @pl.loop(0, BPD)
    def _(b):
        s0[pl.ds(pl.multiple_of(b * BS + BS, BS), BS)] = slip[rows(b * BS, BS)].astype(BF)
        project(s0, co0, b)

    pl.semaphore_wait(barrier, 17)
    sends = []
    for half in range(2):
        sends += gather_copies(0, co0, half)
    halos = halo_copies(0, s0)
    sends += halos
    for copy in sends:
        copy.start()
    load["now"].wait()
    load["rate"].wait()
    own = tab.at[q, core]
    spread_p = [remote(own, own, p_s.at[j], p_r.at[q], col_peers[j]) for j in range(7)]
    for copy in spread_p:
        copy.start()

    load["rank"].wait()
    ri = lax.broadcasted_iota(jnp.int32, (256, 256), 0)
    ci = lax.broadcasted_iota(jnp.int32, (256, 256), 1)
    pm[...] = jnp.where(lax.rem(ri, 32) * 8 + ri // 32 == ci, 1.0, 0.0).astype(BF)
    spread = jnp.where(
        lax.broadcasted_iota(jnp.int32, (8, 256), 1) // 32 == lax.broadcasted_iota(jnp.int32, (8, 256), 0), 1.0, 0.0
    )
    lane = lax.broadcasted_iota(jnp.int32, (16, 8, 256), 2)
    source = lax.broadcasted_iota(jnp.int32, (16, 8, 256), 1) * 128 + col * 8 + lane // 32
    level = lax.rem(lane, 32).astype(F32)

    @pl.loop(0, 8)
    def _(t):
        wide = jnp.dot(
            rank[rows(t * 16, 16)].reshape(128, 8).astype(F32), spread, preferred_element_type=F32
        ).reshape(16, 8, 256)
        target = row * 128 + t * 16 + lax.broadcasted_iota(jnp.int32, (16, 8, 256), 0)
        limit = jnp.where((level < wide) & (jnp.abs(source - target) > 1), wide, 0.0)
        rm[rows(t * 16, 16)] = jnp.concatenate([limit, limit], 1).astype(BF)

    k_of = (
        lax.broadcasted_iota(jnp.int32, (16, 16, 256), 0) * 2 + lax.broadcasted_iota(jnp.int32, (16, 16, 256), 1) // 8
    ).astype(F32).astype(BF)

    @pl.loop(0, 32)
    def _(j):
        @pl.when(j + 3 < 32)
        def _():
            chunk(j + 3).start()

        chunk(j).wait()
        slot = lax.rem(j, 4)
        for b in range(4):
            i = j * 4 + b
            block = buf[slot, b * 256 : (b + 1) * 256].reshape(16, 16, 256)
            masked = jnp.where(k_of < rm[i][None], block, jnp.zeros((), BF)).reshape(256, 256)
            turned = jnp.dot(pm[...], masked, preferred_element_type=F32).astype(BF)
            for u in range(8):
                for half in range(2):
                    at = (half * 8 + u) * 128
                    cm[rows(i * 32, 32), at : at + 128] = turned[u * 32 : (u + 1) * 32, half * 128 : (half + 1) * 128]

    start("state", state_h, state, 9)
    for n in range(3):
        start("near" + str(n), near_h.at[n], nb.at[:, pl.ds(n * 256, 256)], 10 + n)

    def partial_sums(stage, co, rx, rcv):
        def to_partner(d):
            return remote(part.at[d, 1 - core], rx.at[d], b1_s.at[stage, d], b1_r.at[stage, d], partner)

        def to_owner(d):
            return remote(snd.at[d], rcv.at[q], b2_s.at[stage, d], b2_r.at[stage, q], (row, d * 2 + core))

        def combined(d):
            to_partner(d).wait_recv()
            return (part[d, core].astype(F32) + rx[d].astype(F32)).astype(BF)

        def flush(d):
            snd[d] = combined(d)
            to_owner(d).start()

        @pl.loop(0, 8)
        def _(s):
            d = lax.rem(q + 1 + s, 8)
            out = jnp.dot(
                cm[rows(d * 512, 512)], co[...].reshape(2048, ENS), preferred_element_type=F32
            )
            part[d] = out.reshape(2, 256, ENS).astype(BF)
            to_partner(d).start()

            @pl.when(s > 0)
            def _():
                flush(lax.rem(q + s, 8))

        rcv[q] = combined(q)

    def sums_waits(stage, rx, rcv):
        for j in range(1, 8):
            d = lax.rem(q + 8 - j, 8)
            remote(snd.at[d], rcv.at[d], b2_s.at[stage, d], b2_r.at[stage, d], partner).wait_recv()
        total = rcv[0].astype(F32)
        for d in range(1, 8):
            total = total + rcv[d].astype(F32)
        fc[...] = total.astype(BF)

    def sums_drain(stage, rx, rcv):
        for d in range(8):
            remote(part.at[d, 1 - core], rx.at[d], b1_s.at[stage, d], b1_r.at[stage, d], partner).wait_send()
        for j in range(1, 8):
            d = lax.rem(q + j, 8)
            remote(snd.at[d], rcv.at[q], b2_s.at[stage, d], b2_r.at[stage, q], partner).wait_send()

    for half in range(2):
        gather_waits(0, co0, half)
    partial_sums(0, co0, rx0, rcv0)

    for j in range(1, 8):
        d = lax.rem(q + 8 - j, 8)
        remote(tab.at[d, core], tab.at[d, core], p_s.at[0], p_r.at[d], partner).wait_recv()
    share_p = remote(tab.at[:, core], tab.at[:, core], p2_s, p2_r, partner)
    share_p.start()
    load["par"].wait()
    load["adj"].wait()
    load["adjw"].wait()
    slot_of = lax.broadcasted_iota(jnp.int32, (8, 256), 0).astype(F32)

    @pl.loop(0, BPD)
    def _(b):
        s = rows(b * BS, BS)
        p = par[:, s]
        w = jnp.where(slot_of < p[6:7], adjw[:, s], 0.0)
        w = w / jnp.sum(w, axis=0, keepdims=True)
        bricks = adj[:, s]
        hi = (bricks >> 7).astype(F32)
        lo = (bricks & 127).astype(F32)
        mixed = jnp.concatenate(
            [p[0:2], 1.0 / p[2:4], p[3:4] / p[4:5], p[5:6], p[6:8]], 0
        )
        cols[s] = jnp.concatenate([w, hi, lo, mixed], 0).T

    lanes = lax.broadcasted_iota(jnp.int32, (64, 128), 1).astype(F32).astype(BF)
    zero = jnp.zeros((), BF)

    @pl.loop(0, NPAT // 64)
    def _(t):
        s = rows(t * 64, 64)
        c = cols[s]

        def wide(k):
            return jnp.broadcast_to(c[:, k : k + 1], (64, 128)).astype(BF)

        picked = [jnp.where(wide(16 + k) == lanes, wide(k), zero) for k in range(8)]
        group = [wide(8 + k) for k in range(8)]
        for h in range(16):
            v = [jnp.where(group[k] == jnp.asarray(h, BF), picked[k], zero) for k in range(8)]
            wb[s, h * 128 : (h + 1) * 128] = ((v[0] + v[1]) + (v[2] + v[3])) + ((v[4] + v[5]) + (v[6] + v[7]))

    share_p.wait_recv()

    @pl.loop(0, 4)
    def _(t):
        s = rows(t * 512, 512)
        press[s] = jnp.dot(wb[s], tab[...].reshape(2048, 512), preferred_element_type=F32)

    load["state"].wait()
    load["bout"].wait()
    for n in range(3):
        load["near" + str(n)].wait()

    def rates(field, b, pressure, slip_now, state_now):
        s = rows(b * BS, BS)
        near = jnp.dot(nb[s], field[pl.ds(pl.multiple_of(b * BS, BS), 3 * BS)], preferred_element_type=F32)
        far = lax.dot_general(
            bout[:, s], fc[rows(b * R, R)], (((0,), (0,)), ((), ())), preferred_element_type=F32
        )
        c = cols[s]

        def column(k):
            return c[:, 24 + k : 25 + k]

        tau = column(0) - column(5) * slip_now - (near + far)
        sigma = column(1) - pressure
        speed = jnp.exp((tau / sigma - state_now) * column(2))
        drift = column(4) * (jnp.exp((REF_FRICTION - state_now) * column(3)) - speed)
        return speed, drift

    halo_waits(halos, s0)
    sums_waits(0, rx0, rcv0)
    for half in range(2):

        @pl.loop(half * 4, half * 4 + 4)
        def _(b):
            s = rows(b * BS, BS)
            slip_now, state_now = slip[s], state[s]
            speed, drift = rates(s0, b, press[s, 0:ENS], slip_now, state_now)
            acc_s[s] = slip_now + (0.5 * STEP_SIZE) * speed
            acc_t[s] = state_now + (0.5 * STEP_SIZE) * drift
            moved = slip_now + STEP_SIZE * speed
            slip[s] = moved
            state[s] = state_now + STEP_SIZE * drift
            s1[pl.ds(pl.multiple_of(b * BS + BS, BS), BS)] = moved.astype(BF)
            project(s1, co1, b)

        more = gather_copies(1, co1, half)
        for copy in more:
            copy.start()
        sends += more
    halos = halo_copies(1, s1)
    for copy in halos:
        copy.start()
    sends += halos
    sums_drain(0, rx0, rcv0)
    for half in range(2):
        gather_waits(1, co1, half)
    partial_sums(1, co1, rx1, rcv1)
    halo_waits(halos, s1)
    sums_waits(1, rx1, rcv1)

    def outs(b):
        s = rows(b * BS, BS)
        return [
            pltpu.make_async_copy(acc_s.at[s], slip_o.at[s], osem.at[0, b]),
            pltpu.make_async_copy(acc_t.at[s], state_o.at[s], osem.at[1, b]),
        ]

    @pl.loop(0, BPD)
    def _(b):
        s = rows(b * BS, BS)
        pressure = press[s, 0:ENS] + STEP_SIZE * press[s, ENS : 2 * ENS]
        speed, drift = rates(s1, b, pressure, slip[s], state[s])
        acc_s[s] = acc_s[s] + (0.5 * STEP_SIZE) * speed
        acc_t[s] = acc_t[s] + (0.5 * STEP_SIZE) * drift
        for copy in outs(b):
            copy.start()

    sums_drain(1, rx1, rcv1)
    for copy in sends + spread_p + [share_p]:
        copy.wait_send()

    @pl.loop(0, BPD)
    def _(b):
        for copy in outs(b):
            copy.wait()


def per_device(
    slip, state, tau_load, normal_stress, direct_effect, evolution_effect, slip_distance, self_stiffness,
    near_blocks, basis_in, basis_out, coupling, block_rank, adj_bricks, adj_count, adj_weight,
    pressure_now, pressure_rate,
):
    par = jnp.stack(
        [
            tau_load, normal_stress, direct_effect, evolution_effect, slip_distance, self_stiffness,
            adj_count.astype(F32), tau_load,
        ]
    )
    dma = pltpu.SemaphoreType.DMA
    vm = pltpu.VMEM
    scratch = [
        vm((4096, 2048), BF), vm((128, 16, 256), BF), vm((4, 1024, 256), BF), vm((256, 256), BF),
        vm((128, 8, 8), jnp.int32), vm((NPAT, ENS), F32), vm((NPAT, ENS), F32), vm((NPAT, 768), BF),
        vm((R, NPAT), BF), vm((R, NPAT), BF), vm((8, NPAT), jnp.int32), vm((8, NPAT), F32), vm((8, NPAT), F32),
        vm((NPAT, 32), F32), vm((8, 2, 128, 512), BF), vm((NPAT, 2048), BF), vm((NPAT, 512), F32),
        vm((2560, ENS), BF), vm((2560, ENS), BF), vm((2, 8, 128, ENS), BF), vm((2, 8, 128, ENS), BF),
        vm((8, 2, 256, ENS), BF), vm((8, 256, ENS), BF), vm((8, 256, ENS), BF), vm((8, 256, ENS), BF),
        vm((8, 256, ENS), BF), vm((8, 256, ENS), BF), vm((256, ENS), BF), vm((NPAT, ENS), F32), vm((NPAT, ENS), F32),
        dma((13,)), dma((4,)), dma((2, 8)), dma((2, 2, 7)), dma((2, 2, 8)), dma((2, 2)), dma((2, 2)),
        dma((7,)), dma((8,)), dma, dma, dma((2, 8)), dma((2, 8)), dma((2, 8)), dma((2, 8)),
    ]
    anywhere = pl.BlockSpec(memory_space=pl.ANY)
    out = jax.ShapeDtypeStruct((NPAT, ENS), F32)
    return pl.pallas_call(
        kernel,
        out_shape=(out, out),
        in_specs=[anywhere] * 12,
        out_specs=(anywhere, anywhere),
        scratch_shapes=scratch,
        compiler_params=pltpu.CompilerParams(
            collective_id=0, has_side_effects=True, vmem_limit_bytes=67043328
        ),
        name="fault_step",
    )(
        slip, state, par, near_blocks, basis_in, basis_out, coupling.reshape(-1, 256), block_rank,
        adj_bricks, adj_weight, pressure_now, pressure_rate,
    )


def solution(mesh):
    both = ("row", "col")
    vec = P(both)
    mat = P(both, None)
    lanes = P(None, both)
    in_specs = (
        mat, mat, vec, vec, vec, vec, vec, vec, P(None, both, None), lanes, lanes,
        P("row", None, "col"), P("row", None, "col"), lanes, vec, lanes, P("col", None), P("col", None),
    )
    return jax.shard_map(per_device, mesh=mesh, in_specs=in_specs, out_specs=(mat, mat), check_vma=False)
```

time: 663 us -> 109 us (0.16)
  waiting for transfers between devices: 415 us -> 0 us
  local copies, waits for them, and re-layouts: 122 us -> 7.79 us
  Pallas kernels: 0 us -> 99.1 us
  other arithmetic: 51.6 us -> 0.7 us
  matrix products: 47 us -> 0 us
  between operations: 14.5 us -> 0.65 us
  starting transfers between devices: 12.6 us -> 0 us
    all_gather x5 -> x0, waiting for transfers between devices: 216 us -> none  [the longest x2 138 us: stress(): slip_all = lax.all_gather(rounded, 'row', axis=0, tiled=True)]
    psum x2 -> x0, waiting for transfers between devices: 195 us -> none  [stress(): lax.psum(partial_sum.astype(jnp.bfloat16), 'col').astype(jnp.float32)]
    pallas_call x0 -> x1, Pallas kernels: none -> 99.1 us  [per_device(): pl.pallas_call(kernel, out_shape=(out, out), in_specs=[anywhere] * 12, ou...]
    gather x1 -> x0, local copies, waits for them, and re-layouts: 66.4 us -> none  [fault_pressure(): joined[adj_bricks.reshape(slots * patches)]]
    dot_general x13 -> x0, matrix products: 47 us -> none  [the longest x2 19.3 us: stress(): partial_sum = jnp.dot(masked, coeff, preferred_element_type=jnp.float32)]
    unnamed x57 -> x5, local copies, waits for them, and re-layouts: 41.4 us -> 6.27 us
    select_n x5 -> x0, other arithmetic: 22.5 us -> none  [the longest x1 22.4 us: per_device(): masked = jnp.where(keep, matrix, jnp.zeros((), jnp.bfloat16))]
    ppermute x4 -> x0, starting transfers between devices: 12.2 us -> none  [the longest x2 8.32 us: with_halo(): before = lax.ppermute(last, axis, up)]
  transfers between devices with their start and end apart: 11 -> 0, of which waited for: 7 -> 0; matrix products, arithmetic and copies ran while one was open for 28% -> 0% of each run, Pallas kernels for 0% -> 0%
where the time goes in v1:
time: 109 us; the launch traced here: 108 us
  Pallas kernels  99.1 us (91%)
  local copies, waits for them, and re-layouts  7.79 us (7%)
    pallas_call x1, Pallas kernels, per_device(): pl.pallas_call(kernel, out_shape=(out, out), in_specs=[anywhere] * 12, ou...  99.1 us
    unnamed x5, local copies, waits for them, and re-layouts  6.27 us

profile of v1, /device:TPU:1, one launch (start us, length us, event | category | flops | bytes accessed | tf_op | source)
XLA Modules:
  0.0 108.2 jit_solution(6249120829539334635)
XLA Ops:
  0.6 0.7 convert_element_type.3
  1.3 1.5 %stack.32.par_h = f32[8,2048]{1,0:T(8,128)} concatenate(f32[1,2048]{1,0:T(1,128)} %bitcast.9, f32[1,2048]{1,0:T(1,128)} %bitcast.12, f32[1,2048]{1,0:T(1,128)} %bitcast.13, f32[1,2048]{1,0:T(1,128)} %bitcast.14, f32[1,2048]{1,0:T(1,128)} %bitcast.15, f32[1,2048]{1,0:T(1,128)} %bitcast.16, f32[1,2048]{1,0:T(1,128)S(1)} %bitcast.11, f32[1,2048]{1,0:T(1,128)} %bitcast.10), dimensions={0} | concatenate | bytes 131072 | tf_op jit(solution)/shard_map/stack | solution.py:362
  2.8 1.8 %copy.20.rank_h = s32[128,8,8]{2,1,0:T(8,128)} copy(s32[128,8,8]{0,2,1:T(8,128)} %param.30) | data formatting | bytes 65536 | tf_op args[12]
  4.6 99.1 %fault_step.1 = (f32[2048,256]{1,0:T(8,128)}, f32[2048,256]{1,0:T(8,128)}) custom-call(f32[2048,256]{1,0:T(8,128)} %slip_h.1, f32[2048,256]{1,0:T(8,128)} %state_h.1, f32[8,2048]{1,0:T(8,128)} %stack.32.par_h, bf16[3,2048,256]{2,1,0:T(8,128)(2,1)} %near_h.1, bf16[32,2048]{1,0:T(8,128)(2,1)} %bin_h.1, bf16[32,2048]{1,0:T(8,128)(2,1)} %bout_h.1, ...), custom_call_target="tpu_custom_call" | custom-call | tf_op jit(solution)/shard_map/fault_step/pallas_call | solution.py:383
  103.7 0.0 copy-start
  103.7 3.2 %copy.23 = f32[2048,256]{1,0:T(8,128)} copy(f32[2048,256]{1,0:T(8,128)} %get-tuple-element.4) | data formatting | bytes 4194304
  106.9 0.0 copy-done
  106.9 1.3 %copy.24 = f32[2048,256]{1,0:T(8,128)} copy(f32[2048,256]{1,0:T(8,128)S(1)} %copy-done) | data formatting | bytes 4194304
Async XLA Ops:
  103.7 3.2 %copy-start = (f32[2048,256]{1,0:T(8,128)S(1)}, f32[2048,256]{1,0:T(8,128)}, u32[]{:S(2)}) copy-start(f32[2048,256]{1,0:T(8,128)} %get-tuple-element.5) | copy-start | bytes 6291460

commit v2 on v1

v2 whole, which is shorter than its diff:
```python
import jax
import jax.numpy as jnp
from jax import lax
from jax.experimental import pallas as pl
from jax.experimental.pallas import tpu as pltpu
from jax.sharding import PartitionSpec as P

BS = 256
R = 32
BPD = 8
NPAT = 2048
ENS = 256
STEP_SIZE = 0.5
REF_FRICTION = 0.6
BF = jnp.bfloat16
F32 = jnp.float32
MESH = pl.DeviceIdType.MESH
VMEM = 67043328


def rows(start, size):
    return pl.ds(pl.multiple_of(start, size), size)


def kernel(
    slip_h, state_h, near_h, bin_h, bout_h, coup_h, rank_h, adj_h, adjw_h, now_h, rate_h,
    load_h, normal_h, direct_h, evolution_h, distance_h, stiffness_h, count_h,
    slip_o, state_o,
    acc_s, acc_t, cm, rm, buf, pm, pmt, rank, stress, slope, held, sigma, nb, bin_, bout, bt, adj, adjw, par, count, cols, tab, wb,
    s0, s1, co0, co1, part, rx0, rx1, snd, rcv0, rcv1, zsnd, zrcv, fc,
    lsem, csem, osem, a_s, a_r, h_s, h_r, p_s, p_r, p2_s, p2_r, b1_s, b1_r, b2_s, b2_r, z_s, z_r,
):
    row = lax.axis_index("row")
    col = lax.axis_index("col")
    core = lax.rem(col, 2)
    q = col // 2
    g = row * 16 + col
    partner = (row, q * 2 + 1 - core)
    after = lax.rem(g + 1, 128)
    before = lax.rem(g + 127, 128)
    after = (after // 16, lax.rem(after, 16))
    before = (before // 16, lax.rem(before, 16))
    zh, x = q // 4, lax.rem(q, 4)
    across = (row, lax.rem(q + 4, 8) * 2 + core)
    col_peers = [(row, (zh * 4 + lax.rem(x + j, 4)) * 2 + core) for j in range(1, 4)] + [across]

    def remote(src, dst, send, recv, device):
        return pltpu.make_async_remote_copy(
            src_ref=src, dst_ref=dst, send_sem=send, recv_sem=recv, device_id=device, device_id_type=MESH
        )

    def ring(me):
        base = (me // 4) * 4
        up, down = base + lax.rem(me + 1, 4), base + lax.rem(me + 3, 4)
        return lax.rem(me + 4, 8), up, down

    class Gather:
        def __init__(self, piece, me, device, send, recv, relay):
            self.piece, self.device, self.send, self.recv, self.relay = piece, device, send, recv, relay
            other, up, down = ring(me)
            far = (me // 4) * 4 + lax.rem(me + 2, 4)
            self.at = {"me": me, "z": other, "up": up, "down": down, "far": far}
            for name in ("up", "down", "far"):
                self.at["z" + name] = lax.rem(self.at[name] + 4, 8)
            self.open = [name for name in self.at if name != "me"]
            self.sent = []

        def copy(self, which, target, index):
            ref = self.piece(self.at[which])
            return remote(ref, ref, self.send(index), self.recv(self.at[which]), self.device(self.at[target]))

        def put(self, which, target):
            copy = self.copy(which, target, len(self.sent))
            copy.start()
            self.sent.append(copy)

        def got(self, which):
            self.copy(which, "z", 0).wait_recv()
            self.open.remove(which)

        def first(self):
            for target in ("z", "up", "down"):
                self.put("me", target)

        def second(self):
            self.got("z")
            self.put("z", "up")
            self.put("z", "down")

        def third(self):
            back, on = ("up", "down") if self.relay == "down" else ("down", "up")
            self.got(back)
            self.put(back, on)

        def fourth(self):
            back, on = ("down", "up") if self.relay == "up" else ("up", "down")
            self.got("z" + back)
            self.put("z" + back, on)

        def last(self):
            for name in list(self.open):
                self.got(name)

    row_near = [(u, col) for u in ring(row)]
    barrier = pltpu.get_barrier_semaphore()
    for peer in row_near + col_peers + [partner, after, before]:
        pl.semaphore_signal(barrier, inc=1, device_id=peer, device_id_type=MESH)

    def chunk(j):
        slot = lax.rem(j, 8)
        return pltpu.make_async_copy(coup_h.at[rows(j * 1024, 1024)], buf.at[slot], csem.at[slot])

    load = {}

    def start(name, src, dst, index):
        load[name] = pltpu.make_async_copy(src, dst, lsem.at[index])
        load[name].start()

    start("slip", slip_h, acc_s, 0)
    start("bin", bin_h, bin_, 1)
    start("now", now_h, tab.at[q, core, :, pl.ds(0, 256)], 2)
    start("rate", rate_h, tab.at[q, core, :, pl.ds(256, 256)], 3)
    start("rank", rank_h, rank, 4)
    start("adj", adj_h, adj, 5)
    start("adjw", adjw_h, adjw, 6)
    start("count", count_h, count, 7)
    params = (load_h, normal_h, direct_h, evolution_h, distance_h, stiffness_h)
    for n in range(6):
        start("par" + str(n), params[n], par.at[n], 8 + n)
    for j in range(7):
        chunk(j).start()
    start("bout", bout_h, bout, 14)

    def project(field, co, b):
        block = field[pl.ds(pl.multiple_of(b * BS + BS, BS), BS)]
        out = jnp.dot(bin_[:, rows(b * BS, BS)], block, preferred_element_type=F32)
        co[b // 4, row, rows(lax.rem(b, 4) * R, R)] = out.astype(BF)

    def coefficients(stage, co, half):
        return Gather(
            lambda u: co.at[half, u], row, lambda u: (u, col),
            lambda n: a_s.at[stage, half, n], lambda u: a_r.at[stage, half, u],
            ("up", "down")[half],
        )

    def halo_copies(stage, field):
        return [
            remote(field.at[pl.ds(BS, BS)], field.at[pl.ds(9 * BS, BS)], h_s.at[stage, 0], h_r.at[stage, 0], before),
            remote(field.at[pl.ds(8 * BS, BS)], field.at[pl.ds(0, BS)], h_s.at[stage, 1], h_r.at[stage, 1], after),
        ]

    def halo_waits(copies, field):
        for copy in copies:
            copy.wait_recv()

        @pl.when(g == 0)
        def _():
            field[pl.ds(0, BS)] = jnp.zeros((BS, ENS), BF)

        @pl.when(g == 127)
        def _():
            field[pl.ds(9 * BS, BS)] = jnp.zeros((BS, ENS), BF)

    load["slip"].wait()
    load["bin"].wait()

    @pl.loop(0, BPD)
    def _(b):
        s0[pl.ds(pl.multiple_of(b * BS + BS, BS), BS)] = acc_s[rows(b * BS, BS)].astype(BF)
        project(s0, co0, b)

    pl.semaphore_wait(barrier, 10)
    gathers0 = [coefficients(0, co0, half) for half in range(2)]
    for gather in gathers0:
        gather.first()
    halos = halo_copies(0, s0)
    sends = list(halos)
    for copy in halos:
        copy.start()
    load["now"].wait()
    load["rate"].wait()
    bricks_of = Gather(
        lambda u: tab.at[u, core], q, lambda u: (row, u * 2 + core), lambda n: p_s.at[n], lambda u: p_r.at[u],
        "both",
    )
    bricks_of.first()

    load["rank"].wait()
    ri = lax.broadcasted_iota(jnp.int32, (256, 256), 0)
    ci = lax.broadcasted_iota(jnp.int32, (256, 256), 1)
    pm[...] = jnp.where(lax.rem(ri, 32) * 8 + ri // 32 == ci, 1.0, 0.0).astype(BF)
    pmt[...] = jnp.where(lax.rem(ci, 32) * 8 + ci // 32 == ri, 1.0, 0.0).astype(BF)
    spread = jnp.where(
        lax.broadcasted_iota(jnp.int32, (8, 256), 1) // 32 == lax.broadcasted_iota(jnp.int32, (8, 256), 0), 1.0, 0.0
    )
    lane = lax.broadcasted_iota(jnp.int32, (128, 256), 1)
    apart = col * 8 + lane // 32 - row * 128 - lax.broadcasted_iota(jnp.int32, (128, 256), 0)
    level = lax.rem(lane, 32).astype(F32)
    for u in range(8):
        wide = lax.dot_general(
            rank[u].astype(F32), spread, (((0,), (0,)), ((), ())), preferred_element_type=F32
        )
        limit = jnp.where((level < wide) & (jnp.abs(apart + u * 128) > 1), wide, 0.0).astype(BF)
        for t in range(4):
            part[t, 0, u * 32 : (u + 1) * 32] = limit[t * 32 : (t + 1) * 32]
    for t in range(4):
        limit = jnp.dot(pmt[...], part[t, 0], preferred_element_type=F32).reshape(32, 8, 256)
        rm[t * 32 : (t + 1) * 32] = jnp.concatenate([limit, limit], 1).astype(BF)

    for name in ["adj", "adjw", "count"] + ["par" + str(n) for n in range(6)]:
        load[name].wait()
    slot_of = lax.broadcasted_iota(jnp.int32, (8, 128), 0)

    @pl.loop(0, 16)
    def _(t):
        s = rows(t * 128, 128)
        used = count[pl.ds(t, 1)]
        w = jnp.where(slot_of < used, adjw[:, s], 0.0)
        w = w / jnp.sum(w, axis=0, keepdims=True)
        bricks = adj[:, s]
        hi = (bricks >> 7).astype(F32)
        lo = (bricks & 127).astype(F32)
        p = [par[n, pl.ds(t, 1)] for n in range(6)]
        mixed = [p[0], p[1], 1.0 / p[2], 1.0 / p[3], p[3] / p[4], p[5], p[0], p[1]]
        cols[s] = jnp.concatenate([w, hi, lo] + mixed, 0).T

    lanes = lax.broadcasted_iota(jnp.int32, (16, 128), 1).astype(F32).astype(BF)
    zero = jnp.zeros((), BF)

    def one_hot(t):
        s = rows(t * 16, 16)
        c = cols[s]

        def wide(k):
            return jnp.broadcast_to(c[:, k : k + 1], (16, 128)).astype(BF)

        picked = [jnp.where(wide(16 + k) == lanes, wide(k), zero) for k in range(8)]
        group = [wide(8 + k) for k in range(8)]
        for h in range(16):
            v = [jnp.where(group[k] == jnp.asarray(h, BF), picked[k], zero) for k in range(8)]
            wb[s, h * 128 : (h + 1) * 128] = ((v[0] + v[1]) + (v[2] + v[3])) + ((v[4] + v[5]) + (v[6] + v[7]))

    k_of = (
        lax.broadcasted_iota(jnp.int32, (16, 16, 256), 0) * 2 + lax.broadcasted_iota(jnp.int32, (16, 16, 256), 1) // 8
    ).astype(F32).astype(BF)

    def mask_chunk(j):
        @pl.when(j + 7 < 32)
        def _():
            chunk(j + 7).start()

        chunk(j).wait()
        slot = lax.rem(j, 8)
        for b in range(4):
            i = j * 4 + b
            block = buf[slot, b * 256 : (b + 1) * 256].reshape(16, 16, 256)
            masked = jnp.where(k_of < rm[i][None], block, jnp.zeros((), BF)).reshape(256, 256)
            turned = jnp.dot(pm[...], masked, preferred_element_type=F32).astype(BF)
            one_hot(i)
            for u in range(8):
                for half in range(2):
                    at = (half * 8 + u) * 128
                    cm[rows(i * 32, 32), at : at + 128] = turned[u * 32 : (u + 1) * 32, half * 128 : (half + 1) * 128]

    def step(gathers, name):
        for gather in gathers:
            getattr(gather, name)()

    pl.loop(0, 8)(mask_chunk)
    for name in ("second", "third"):
        step(gathers0, name)
    for name in ("second", "third"):
        step([bricks_of], name)
    pl.loop(8, 16)(mask_chunk)
    step(gathers0, "fourth")
    pl.loop(16, 22)(mask_chunk)
    step([bricks_of], "fourth")
    pl.loop(22, 32)(mask_chunk)

    start("state", state_h, acc_t, 15)
    for n in range(3):
        start("near" + str(n), near_h.at[n], nb.at[:, pl.ds(n * 256, 256)], 16 + n)

    def dest(s):
        return lax.rem(zh + 1 + s // 4, 2) * 4 + lax.rem(x + 1 + lax.rem(s, 4), 4)

    def to_partner(stage, d, rx):
        return remote(part.at[d, 1 - core], rx.at[d], b1_s.at[stage, d], b1_r.at[stage, d], partner)

    def to_owner(stage, s, rcv):
        slot = (s // 4) * 4 + x
        owner = (row, (zh * 4 + lax.rem(x + 1 + lax.rem(s, 4), 4)) * 2 + core)
        return remote(snd.at[dest(s)], rcv.at[slot], b2_s.at[stage, dest(s)], b2_r.at[stage, slot], owner)

    def to_across(stage):
        return remote(zsnd.at[stage], zrcv.at[stage], z_s.at[stage], z_r.at[stage], across)

    def partial_sums(stage, co, rx, rcv):
        def combined(d):
            to_partner(stage, d, rx).wait_recv()
            return (part[d, core].astype(F32) + rx[d].astype(F32)).astype(BF)

        def flush(s):
            snd[dest(s)] = combined(dest(s))
            to_owner(stage, s, rcv).start()

        @pl.loop(0, 8)
        def _(s):
            d = dest(s)
            out = jnp.dot(
                cm[rows(d * 512, 512)], co[...].reshape(2048, ENS), preferred_element_type=F32
            )
            part[d] = out.reshape(2, 256, ENS).astype(BF)
            to_partner(stage, d, rx).start()

            @pl.when((s > 1) & (s != 5))
            def _():
                flush(s - 2)

        flush(6)
        rcv[x] = combined(dest(3))
        rcv[4 + x] = combined(dest(7))

    def arrived(stage, group, rcv):
        for j in range(1, 4):
            slot = group * 4 + lax.rem(x + j, 4)
            remote(snd.at[0], rcv.at[slot], b2_s.at[stage, 0], b2_r.at[stage, slot], partner).wait_recv()
        total = rcv[group * 4].astype(F32)
        for j in range(1, 4):
            total = total + rcv[group * 4 + j].astype(F32)
        return total

    def sums_across(stage, rcv):
        zsnd[stage] = arrived(stage, 0, rcv).astype(BF)
        to_across(stage).start()

    def sums_waits(stage, rcv):
        total = arrived(stage, 1, rcv)
        to_across(stage).wait_recv()
        fc[...] = (total + zrcv[stage].astype(F32)).astype(BF)

    def sums_drain(stage, rx, rcv):
        for d in range(8):
            to_partner(stage, d, rx).wait_send()
        for s in (0, 1, 2, 4, 5, 6):
            to_owner(stage, s, rcv).wait_send()
        to_across(stage).wait_send()

    step([bricks_of], "last")
    share_p = remote(tab.at[:, core], tab.at[:, core], p2_s, p2_r, partner)
    share_p.start()
    step(gathers0, "last")
    partial_sums(0, co0, rx0, rcv0)

    def pressures(t, which):
        s = rows(t * 512, 512)
        at = which * ENS
        field = jnp.dot(wb[s], tab[:, :, :, at : at + ENS].reshape(2048, ENS), preferred_element_type=F32)
        if which == 0:
            stiff = cols[s][:, 25:26] - field
            sigma[s] = stiff
        else:
            stiff = sigma[s] - STEP_SIZE * field
        slope[s] = cols[s][:, 26:27] / stiff

    def column(s, k):
        return cols[s][:, 24 + k : 25 + k]

    def before_far(field, b, slip_now, state_now):
        s = rows(b * BS, BS)
        near = jnp.dot(nb[s], field[pl.ds(pl.multiple_of(b * BS, BS), 3 * BS)], preferred_element_type=F32)
        stress[s] = column(s, 0) - column(s, 5) * slip_now - near
        return column(s, 4) * jnp.exp((REF_FRICTION - state_now) * column(s, 3))

    def far_part(b):
        return jnp.dot(bt[rows(b * BS, BS), 0:R], fc[rows(b * R, R)], preferred_element_type=F32)

    load["state"].wait()
    load["bout"].wait()
    for n in range(3):
        load["near" + str(n)].wait()
    share_p.wait_recv()
    pl.loop(0, 4)(lambda t: pressures(t, 0))
    sums_across(0, rcv0)
    for b in range(BPD):
        bt[b * BS : (b + 1) * BS, 0:R] = bout[:, b * BS : (b + 1) * BS].astype(F32).T.astype(BF)
    halo_waits(halos, s0)

    @pl.loop(0, BPD)
    def _(b):
        s = rows(b * BS, BS)
        held[s] = before_far(s0, b, acc_s[s], acc_t[s])

    sums_waits(0, rcv0)
    gathers1 = [coefficients(1, co1, half) for half in range(2)]
    for half in range(2):

        @pl.loop(half * 4, half * 4 + 4)
        def _(b):
            s = rows(b * BS, BS)
            slip_now, state_now = acc_s[s], acc_t[s]
            speed = jnp.exp((stress[s] - far_part(b)) * slope[s] - state_now * column(s, 2))
            drift = held[s] - column(s, 4) * speed
            moved = slip_now + STEP_SIZE * speed
            stress[s] = moved
            s1[pl.ds(pl.multiple_of(b * BS + BS, BS), BS)] = moved.astype(BF)
            held[s] = state_now + STEP_SIZE * drift
            acc_s[s] = slip_now + (0.5 * STEP_SIZE) * speed
            acc_t[s] = state_now + (0.5 * STEP_SIZE) * drift
            project(s1, co1, b)

        gathers1[half].first()

    halos = halo_copies(1, s1)
    for copy in halos:
        copy.start()
    sends += halos
    pl.loop(0, 4)(lambda t: pressures(t, 1))
    step(gathers1, "second")
    step(gathers1, "third")
    halo_waits(halos, s1)

    def before_far_1(b):
        s = rows(b * BS, BS)
        state_now = held[s]
        back = before_far(s1, b, stress[s], state_now)
        acc_t[s] = acc_t[s] + (0.5 * STEP_SIZE) * back
        held[s] = state_now * column(s, 2)

    pl.loop(0, 5)(before_far_1)
    step(gathers1, "fourth")
    pl.loop(5, BPD)(before_far_1)
    sums_drain(0, rx0, rcv0)
    step(gathers1, "last")
    partial_sums(1, co1, rx1, rcv1)
    sums_across(1, rcv1)
    sums_waits(1, rcv1)

    def outs(b):
        s = rows(b * BS, BS)
        return [
            pltpu.make_async_copy(acc_s.at[s], slip_o.at[s], osem.at[0, b]),
            pltpu.make_async_copy(acc_t.at[s], state_o.at[s], osem.at[1, b]),
        ]

    @pl.loop(0, BPD)
    def _(b):
        s = rows(b * BS, BS)
        speed = jnp.exp((stress[s] - far_part(b)) * slope[s] - held[s])
        acc_s[s] = acc_s[s] + (0.5 * STEP_SIZE) * speed
        acc_t[s] = acc_t[s] - (0.5 * STEP_SIZE) * (column(s, 4) * speed)
        for copy in outs(b):
            copy.start()

    sums_drain(1, rx1, rcv1)
    for gather in gathers0 + [bricks_of] + gathers1:
        sends += gather.sent
    for copy in sends + [share_p]:
        copy.wait_send()

    @pl.loop(0, BPD)
    def _(b):
        for copy in outs(b):
            copy.wait()


def per_device(
    slip, state, tau_load, normal_stress, direct_effect, evolution_effect, slip_distance, self_stiffness,
    near_blocks, basis_in, basis_out, coupling, block_rank, adj_bricks, adj_count, adj_weight,
    pressure_now, pressure_rate,
):
    dma = pltpu.SemaphoreType.DMA
    vm = pltpu.VMEM
    scratch = [
        vm((NPAT, ENS), F32), vm((NPAT, ENS), F32), vm((4096, 2048), BF), vm((128, 16, 256), BF), vm((8, 1024, 256), BF), vm((256, 256), BF), vm((256, 256), BF),
        vm((8, 8, 128), jnp.int32), vm((NPAT, ENS), F32), vm((NPAT, ENS), F32), vm((NPAT, ENS), F32),
        vm((NPAT, ENS), F32), vm((NPAT, 768), BF),
        vm((R, NPAT), BF), vm((R, NPAT), BF), vm((NPAT, 128), BF), vm((8, NPAT), jnp.int32), vm((8, NPAT), F32), vm((6, 16, 128), F32),
        vm((16, 128), jnp.int32), vm((NPAT, 32), F32), vm((8, 2, 128, 512), BF), vm((NPAT, 2048), BF),
        vm((2560, ENS), BF), vm((2560, ENS), BF), vm((2, 8, 128, ENS), BF), vm((2, 8, 128, ENS), BF),
        vm((8, 2, 256, ENS), BF), vm((8, 256, ENS), BF), vm((8, 256, ENS), BF), vm((8, 256, ENS), BF),
        vm((8, 256, ENS), BF), vm((8, 256, ENS), BF), vm((2, 256, ENS), BF), vm((2, 256, ENS), BF),
        vm((256, ENS), BF), dma((19,)), dma((8,)), dma((2, 8)), dma((2, 2, 7)), dma((2, 2, 8)), dma((2, 2)), dma((2, 2)),
        dma((7,)), dma((8,)), dma, dma, dma((2, 8)), dma((2, 8)), dma((2, 8)), dma((2, 8)), dma((2,)), dma((2,)),
    ]
    anywhere = pl.BlockSpec(memory_space=pl.ANY)
    out = jax.ShapeDtypeStruct((NPAT, ENS), F32)
    return pl.pallas_call(
        kernel,
        out_shape=(out, out),
        in_specs=[anywhere] * 18,
        out_specs=(anywhere, anywhere),
        scratch_shapes=scratch,
        compiler_params=pltpu.CompilerParams(
            collective_id=0, has_side_effects=True, vmem_limit_bytes=VMEM
        ),
        name="fault_step",
    )(
        slip, state, near_blocks, basis_in, basis_out, coupling.reshape(-1, 256), block_rank.transpose(1, 2, 0),
        adj_bricks, adj_weight, pressure_now, pressure_rate,
        *[
            v.reshape(16, 128)
            for v in (
                tau_load, normal_stress, direct_effect, evolution_effect, slip_distance, self_stiffness, adj_count
            )
        ],
    )


def solution(mesh):
    both = ("row", "col")
    vec = P(both)
    mat = P(both, None)
    lanes = P(None, both)
    in_specs = (
        mat, mat, vec, vec, vec, vec, vec, vec, P(None, both, None), lanes, lanes,
        P("row", None, "col"), P("row", None, "col"), lanes, vec, lanes, P("col", None), P("col", None),
    )
    return jax.shard_map(per_device, mesh=mesh, in_specs=in_specs, out_specs=(mat, mat), check_vma=False)
```

time: 109 us -> 86.7 us (0.80)
  Pallas kernels: 99.1 us -> 81.4 us
  local copies, waits for them, and re-layouts: 7.79 us -> 4.52 us
    pallas_call x1, Pallas kernels: 99.1 us -> 81.4 us  [per_device(): pl.pallas_call(kernel, out_shape=(out, out), in_specs=[anywhere] * 18, ou...]
    unnamed x5 -> x4, local copies, waits for them, and re-layouts: 6.27 us -> 4.52 us
    another operation x1 -> x0, local copies, waits for them, and re-layouts: 1.52 us -> none  [per_device(): jnp.stack([tau_load, normal_stress, direct_effect, evolution_effect, slip...]
where the time goes in v2:
time: 86.7 us; the launch traced here: 86.6 us
  Pallas kernels  81.4 us (94%)
  local copies, waits for them, and re-layouts  4.52 us (5%)
    pallas_call x1, Pallas kernels, per_device(): pl.pallas_call(kernel, out_shape=(out, out), in_specs=[anywhere] * 18, ou...  81.4 us
    unnamed x4, local copies, waits for them, and re-layouts  4.52 us

profile of v2, /device:TPU:1, one launch (start us, length us, event | category | flops | bytes accessed | tf_op | source)
XLA Modules:
  0.0 86.6 jit_solution(15749446272593611792)
XLA Ops:
  0.6 81.4 %fault_step.1 = (f32[2048,256]{1,0:T(8,128)}, f32[2048,256]{1,0:T(8,128)}) custom-call(f32[2048,256]{1,0:T(8,128)} %slip_h.1, f32[2048,256]{1,0:T(8,128)} %state_h.1, bf16[3,2048,256]{2,1,0:T(8,128)(2,1)} %near_h.1, bf16[32,2048]{1,0:T(8,128)(2,1)} %bin_h.1, bf16[32,2048]{1,0:T(8,128)(2,1)} %bout_h.1, bf16[32768,256]{1,0:T(8,128)(2,1)} %bitcast.9, ...), custom_call_target="tpu_custom_call" | custom-call | tf_op jit(solution)/shard_map/fault_step/pallas_call | solution.py:488
  82.1 0.0 copy-start
  82.1 3.2 %copy.22 = f32[2048,256]{1,0:T(8,128)} copy(f32[2048,256]{1,0:T(8,128)} %get-tuple-element.4) | data formatting | bytes 4194304
  85.3 0.0 copy-done
  85.3 1.3 %copy.23 = f32[2048,256]{1,0:T(8,128)} copy(f32[2048,256]{1,0:T(8,128)S(1)} %copy-done) | data formatting | bytes 4194304
Async XLA Ops:
  82.1 3.2 %copy-start = (f32[2048,256]{1,0:T(8,128)S(1)}, f32[2048,256]{1,0:T(8,128)}, u32[]{:S(2)}) copy-start(f32[2048,256]{1,0:T(8,128)} %get-tuple-element.5) | copy-start | bytes 6291460

commit v3 on v2

--- a/solution.py
+++ b/solution.py
@@ -116,10 +116,10 @@
         load[name] = pltpu.make_async_copy(src, dst, lsem.at[index])
         load[name].start()
 
+    start("now", now_h, tab.at[q, core, :, pl.ds(0, 256)], 2)
+    start("rate", rate_h, tab.at[q, core, :, pl.ds(256, 256)], 3)
     start("slip", slip_h, acc_s, 0)
     start("bin", bin_h, bin_, 1)
-    start("now", now_h, tab.at[q, core, :, pl.ds(0, 256)], 2)
-    start("rate", rate_h, tab.at[q, core, :, pl.ds(256, 256)], 3)
     start("rank", rank_h, rank, 4)
     start("adj", adj_h, adj, 5)
     start("adjw", adjw_h, adjw, 6)
@@ -161,6 +161,15 @@
         def _():
             field[pl.ds(9 * BS, BS)] = jnp.zeros((BS, ENS), BF)
 
+    load["now"].wait()
+    load["rate"].wait()
+    pl.semaphore_wait(barrier, 10)
+    bricks_of = Gather(
+        lambda u: tab.at[u, core], q, lambda u: (row, u * 2 + core), lambda n: p_s.at[n], lambda u: p_r.at[u],
+        "both",
+    )
+    bricks_of.first()
+
     load["slip"].wait()
     load["bin"].wait()
 
@@ -169,7 +178,6 @@
         s0[pl.ds(pl.multiple_of(b * BS + BS, BS), BS)] = acc_s[rows(b * BS, BS)].astype(BF)
         project(s0, co0, b)
 
-    pl.semaphore_wait(barrier, 10)
     gathers0 = [coefficients(0, co0, half) for half in range(2)]
     for gather in gathers0:
         gather.first()
@@ -177,14 +185,6 @@
     sends = list(halos)
     for copy in halos:
         copy.start()
-    load["now"].wait()
-    load["rate"].wait()
-    bricks_of = Gather(
-        lambda u: tab.at[u, core], q, lambda u: (row, u * 2 + core), lambda n: p_s.at[n], lambda u: p_r.at[u],
-        "both",
-    )
-    bricks_of.first()
-
     load["rank"].wait()
     ri = lax.broadcasted_iota(jnp.int32, (256, 256), 0)
     ci = lax.broadcasted_iota(jnp.int32, (256, 256), 1)
@@ -256,7 +256,8 @@
             block = buf[slot, b * 256 : (b + 1) * 256].reshape(16, 16, 256)
             masked = jnp.where(k_of < rm[i][None], block, jnp.zeros((), BF)).reshape(256, 256)
             turned = jnp.dot(pm[...], masked, preferred_element_type=F32).astype(BF)
-            one_hot(i)
+            if b < 3:
+                one_hot(j * 3 + b)
             for u in range(8):
                 for half in range(2):
                     at = (half * 8 + u) * 128
@@ -266,16 +267,14 @@
         for gather in gathers:
             getattr(gather, name)()
 
-    pl.loop(0, 8)(mask_chunk)
-    for name in ("second", "third"):
-        step(gathers0, name)
+    pl.loop(0, 10)(mask_chunk)
     for name in ("second", "third"):
         step([bricks_of], name)
-    pl.loop(8, 16)(mask_chunk)
+        step(gathers0, name)
+    pl.loop(10, 21)(mask_chunk)
+    step([bricks_of], "fourth")
     step(gathers0, "fourth")
-    pl.loop(16, 22)(mask_chunk)
-    step([bricks_of], "fourth")
-    pl.loop(22, 32)(mask_chunk)
+    pl.loop(21, 32)(mask_chunk)
 
     start("state", state_h, acc_t, 15)
     for n in range(3):
@@ -351,6 +350,13 @@
     share_p.start()
     step(gathers0, "last")
     partial_sums(0, co0, rx0, rcv0)
+
+    def one_hot_rest(t):
+        for n in range(4):
+            one_hot(t * 4 + n)
+
+    pl.loop(24, 32)(one_hot_rest)
+    sums_across(0, rcv0)
 
     def pressures(t, which):
         s = rows(t * 512, 512)
@@ -381,7 +387,6 @@
         load["near" + str(n)].wait()
     share_p.wait_recv()
     pl.loop(0, 4)(lambda t: pressures(t, 0))
-    sums_across(0, rcv0)
     for b in range(BPD):
         bt[b * BS : (b + 1) * BS, 0:R] = bout[:, b * BS : (b + 1) * BS].astype(F32).T.astype(BF)
     halo_waits(halos, s0)

time: 86.7 us -> 84.8 us (0.978)
  Pallas kernels: 81.4 us -> 78.8 us
    pallas_call x1, Pallas kernels: 81.4 us -> 78.8 us  [per_device(): pl.pallas_call(kernel, out_shape=(out, out), in_specs=[anywhere] * 18, ou...]
where the time goes in v3:
time: 84.8 us; the launch traced here: 84 us
  Pallas kernels  78.8 us (93%)
  local copies, waits for them, and re-layouts  4.52 us (5%)
    pallas_call x1, Pallas kernels, per_device(): pl.pallas_call(kernel, out_shape=(out, out), in_specs=[anywhere] * 18, ou...  78.8 us
    unnamed x4, local copies, waits for them, and re-layouts  4.52 us

profile of v3, /device:TPU:1, one launch (start us, length us, event | category | flops | bytes accessed | tf_op | source)
XLA Modules:
  0.0 84.0 jit_solution(16051523991962441352)
XLA Ops:
  0.6 78.8 %fault_step.1 = (f32[2048,256]{1,0:T(8,128)}, f32[2048,256]{1,0:T(8,128)}) custom-call(f32[2048,256]{1,0:T(8,128)} %slip_h.1, f32[2048,256]{1,0:T(8,128)} %state_h.1, bf16[3,2048,256]{2,1,0:T(8,128)(2,1)} %near_h.1, bf16[32,2048]{1,0:T(8,128)(2,1)} %bin_h.1, bf16[32,2048]{1,0:T(8,128)(2,1)} %bout_h.1, bf16[32768,256]{1,0:T(8,128)(2,1)} %bitcast.9, ...), custom_call_target="tpu_custom_call" | custom-call | tf_op jit(solution)/shard_map/fault_step/pallas_call | solution.py:493
  79.5 0.0 copy-start
  79.5 3.2 %copy.22 = f32[2048,256]{1,0:T(8,128)} copy(f32[2048,256]{1,0:T(8,128)} %get-tuple-element.4) | data formatting | bytes 4194304
  82.7 0.0 copy-done
  82.7 1.3 %copy.23 = f32[2048,256]{1,0:T(8,128)} copy(f32[2048,256]{1,0:T(8,128)S(1)} %copy-done) | data formatting | bytes 4194304
Async XLA Ops:
  79.5 3.2 %copy-start = (f32[2048,256]{1,0:T(8,128)S(1)}, f32[2048,256]{1,0:T(8,128)}, u32[]{:S(2)}) copy-start(f32[2048,256]{1,0:T(8,128)} %get-tuple-element.5) | copy-start | bytes 6291460

commit v4 on v3

--- a/solution.py
+++ b/solution.py
@@ -356,7 +356,6 @@
             one_hot(t * 4 + n)
 
     pl.loop(24, 32)(one_hot_rest)
-    sums_across(0, rcv0)
 
     def pressures(t, which):
         s = rows(t * 512, 512)
@@ -387,6 +386,7 @@
         load["near" + str(n)].wait()
     share_p.wait_recv()
     pl.loop(0, 4)(lambda t: pressures(t, 0))
+    sums_across(0, rcv0)
     for b in range(BPD):
         bt[b * BS : (b + 1) * BS, 0:R] = bout[:, b * BS : (b + 1) * BS].astype(F32).T.astype(BF)
     halo_waits(halos, s0)

time: 84.8 us -> 85.5 us (level)
  no operation moved by 1% of the time
where the time goes in v4:
time: 85.5 us; the launch traced here: 84 us
  Pallas kernels  78.8 us (92%)
  local copies, waits for them, and re-layouts  4.52 us (5%)
    pallas_call x1, Pallas kernels, per_device(): pl.pallas_call(kernel, out_shape=(out, out), in_specs=[anywhere] * 18, ou...  78.8 us
    unnamed x4, local copies, waits for them, and re-layouts  4.52 us

profile of v4, /device:TPU:1, one launch (start us, length us, event | category | flops | bytes accessed | tf_op | source)
XLA Modules:
  0.0 84.0 jit_solution(7814755436580323108)
XLA Ops:
  0.6 78.8 %fault_step.1 = (f32[2048,256]{1,0:T(8,128)}, f32[2048,256]{1,0:T(8,128)}) custom-call(f32[2048,256]{1,0:T(8,128)} %slip_h.1, f32[2048,256]{1,0:T(8,128)} %state_h.1, bf16[3,2048,256]{2,1,0:T(8,128)(2,1)} %near_h.1, bf16[32,2048]{1,0:T(8,128)(2,1)} %bin_h.1, bf16[32,2048]{1,0:T(8,128)(2,1)} %bout_h.1, bf16[32768,256]{1,0:T(8,128)(2,1)} %bitcast.9, ...), custom_call_target="tpu_custom_call" | custom-call | tf_op jit(solution)/shard_map/fault_step/pallas_call | solution.py:493
  79.5 0.0 copy-start
  79.5 3.2 %copy.22 = f32[2048,256]{1,0:T(8,128)} copy(f32[2048,256]{1,0:T(8,128)} %get-tuple-element.4) | data formatting | bytes 4194304
  82.7 0.0 copy-done
  82.7 1.3 %copy.23 = f32[2048,256]{1,0:T(8,128)} copy(f32[2048,256]{1,0:T(8,128)S(1)} %copy-done) | data formatting | bytes 4194304
Async XLA Ops:
  79.5 3.2 %copy-start = (f32[2048,256]{1,0:T(8,128)S(1)}, f32[2048,256]{1,0:T(8,128)}, u32[]{:S(2)}) copy-start(f32[2048,256]{1,0:T(8,128)} %get-tuple-element.5) | copy-start | bytes 6291460
